TPU v7x, 32 devices: a whole 2x2x4 slice. The times are simulated.
32 devices in a mesh: gx: 16 (over z, y, x), gy: 2 (over core).
Axes of the slice: x: 2, y: 2, z: 4, core: 2. Of those that a mesh axis runs over, the one named last changes fastest.
Arguments:
- density: float32 [128, 32, 64], P('gx', None, 'gy'), may hold values from 0.5 to 1.5
- momentum: float32 [3, 128, 32, 64], P(None, 'gx', None, 'gy'), may hold values from -3 to 3
- energy: float32 [128, 32, 64], P('gx', None, 'gy'), may hold values from 2.5 to 4
- eddy_normal_cell: int32 [1024], P('gx'), may hold values from 0 to 63
- eddy_spanwise_cell: int32 [1024], P('gx'), may hold values from 0 to 31
- eddy_signs: int32 [1024, 3], P('gx'), may hold values from 0 to 1
- eddy_strengths: float32 [1024], P('gx'), may hold values from 0.3 to 3
- filter_matrices: float32 [1, 128, 128], replicated, may hold values from -1.25 to 1.25
- shock_switch: int32 [1, 64], P(None, 'gy'), may hold values 0 or 1
- dilatation_bin: int32 [128, 32, 64], P('gx', None, 'gy'), may hold values from 0 to 63
- vorticity_bin: int32 [128, 32, 64], P('gx', None, 'gy'), may hold values from 0 to 63, as said below
Outputs:
- conserved_next: float32 [5, 128, 32, 64], P(None, 'gx', None, 'gy')
- histogram: float32 [64, 64], replicated
Inputs may be any that keep to these rules, and one draw needn't show every extreme that they name: vorticity_bin at streamwise cell x is x * 64 // 128 or one more, modulo 64.
All inputs are finite; a program needn't handle non-finite values. No bound on the sum of `shock_switch` on one device may be relied on, other than what follows from the above.
Results may differ from a plain program's by a relative error of at most 0.0003.
Values sent between devices are 32-bit elements; how exact they have to be, the bound alone decides.
No kernel may reach another device: no remote copies, remote signals or barrier semaphores. Data moves between devices by JAX's collectives and lax.ppermute only.
A program may use at most 64 MiB of HBM per device.

v0:
```python
import math
import jax
import jax.numpy as jnp
from jax import lax
from jax.sharding import PartitionSpec as P

HISTOGRAM_BINS = 64
SIGMA_Y = 32
SIGMA_Z = 8
TIME_STEP = 0.1
GAMMA_GAS = 1.4
SENSOR_EPS = 0.1
HAT_PEAK = math.sqrt(1.5)


def extended(x, sides, width):
    for axis, dim in sides:
        size, length = (lax.axis_size(axis), x.shape[dim])
        up = [(i, (i + 1) % size) for i in range(size - 1)]
        down = [(j, i) for i, j in up]
        last = lax.slice_in_dim(x, length - width, length, axis=dim)
        first = lax.slice_in_dim(x, 0, width, axis=dim)
        before = lax.ppermute(last, axis, up)
        after = lax.ppermute(first, axis, down)
        x = jnp.concatenate([before, x, after], axis=dim)
    return x


def hat_shape(centres, coords, spread, period):
    offset = coords[None, :] - centres[:, None]
    if period > 0:
        offset = jnp.mod(offset + period / 2, period) - period / 2
    return HAT_PEAK * jnp.maximum(0.0, 1.0 - jnp.abs(offset) / spread)


def inflow_from(centre_y, centre_z, eddy_weight, coords_y, coords_z, span):
    shape_y = hat_shape(centre_y, coords_y, float(SIGMA_Y), 0)
    shape_z = hat_shape(centre_z, coords_z, float(SIGMA_Z), span)
    weighted = (eddy_weight[:, :, None] * shape_z[:, None, :]).reshape(eddy_weight.shape[0], -1)
    inflow = jnp.dot(weighted.T, shape_y, precision=lax.Precision.HIGHEST)
    return inflow.reshape(3, coords_z.shape[0], coords_y.shape[0])


def ghost_state(inflow):
    mom_x = 1.0 + inflow[0]
    kinetic = mom_x * mom_x + inflow[1] * inflow[1] + inflow[2] * inflow[2]
    return jnp.stack([jnp.ones_like(mom_x), mom_x, inflow[1], inflow[2], 3.0 + 0.5 * kinetic])


def flux_of(fields, velocity, pressure, direction):
    result = fields * velocity[direction][None]
    result = result.at[1 + direction].add(pressure)
    return result.at[4].add(pressure * velocity[direction])


def central_x(values):
    return (values[..., 2:, :, 1:-1] - values[..., :-2, :, 1:-1]) * 0.5


def central_y(values):
    return (values[..., 1:-1, :, 2:] - values[..., 1:-1, :, :-2]) * 0.5


def central_z(values):
    centre = values[..., 1:-1, :, 1:-1]
    return (jnp.roll(centre, -1, axis=-2) - jnp.roll(centre, 1, axis=-2)) * 0.5


def section_rhs(padded):
    velocity = padded[1:4] / padded[0][None]
    pressure = (GAMMA_GAS - 1.0) * (padded[4] - 0.5 * jnp.sum(padded[1:4] * velocity, axis=0))
    change = central_x(flux_of(padded, velocity, pressure, 0))
    change = change + central_y(flux_of(padded, velocity, pressure, 1))
    change = change + central_z(flux_of(padded, velocity, pressure, 2))
    updated = padded[:, 1:-1, :, 1:-1] - TIME_STEP * change
    dilatation = central_x(velocity[0]) + central_y(velocity[1]) + central_z(velocity[2])
    vort_x = central_y(velocity[2]) - central_z(velocity[1])
    vort_y = central_z(velocity[0]) - central_x(velocity[2])
    vort_z = central_x(velocity[1]) - central_y(velocity[0])
    squared = dilatation * dilatation
    shock_sensor = squared / (
        squared + vort_x * vort_x + vort_y * vort_y + vort_z * vort_z + SENSOR_EPS
    )
    return (updated, shock_sensor)


def filter_lines(pencil, filter_matrices):
    block_count, block_len = (filter_matrices.shape[0], filter_matrices.shape[1])
    lanes = pencil.shape[2]
    blocks = pencil.reshape(5, block_count, block_len, lanes)
    smooth = jnp.einsum("bij,fbjp->fbip", filter_matrices, blocks, precision=lax.Precision.HIGHEST)
    return smooth.reshape(5, block_count * block_len, lanes)


def plane_histogram(shock_sensor, dilatation_bin, vorticity_bin):
    bin_levels = jnp.arange(HISTOGRAM_BINS, dtype=jnp.int32)

    def accumulate_plane(histogram_totals, histogram_parts):
        sensor_plane, plane_dilatation, plane_vorticity = histogram_parts
        flat_sensor = sensor_plane.reshape(-1)
        dilatation_table = (plane_dilatation.reshape(-1)[None, :] == bin_levels[:, None]).astype(
            jnp.float32
        )
        vorticity_table = jnp.where(
            plane_vorticity.reshape(-1)[:, None] == bin_levels[None, :], flat_sensor[:, None], 0.0
        )
        return (
            histogram_totals
            + jnp.dot(dilatation_table, vorticity_table, precision=lax.Precision.HIGHEST),
            None,
        )

    histogram_totals, _ = lax.scan(
        accumulate_plane,
        jnp.zeros((HISTOGRAM_BINS, HISTOGRAM_BINS), jnp.float32),
        (shock_sensor, dilatation_bin, vorticity_bin),
    )
    return histogram_totals


def shards(
    density,
    momentum,
    energy,
    eddy_normal_cell,
    eddy_spanwise_cell,
    eddy_signs,
    eddy_strengths,
    filter_matrices,
    shock_switch,
    dilatation_bin,
    vorticity_bin,
):
    cells_x, span, cells_y = density.shape
    slab_index = lax.axis_index("gx")
    block_index = lax.axis_index("gy")
    slab_count = lax.axis_size("gx")
    fields = jnp.concatenate([density[None], momentum, energy[None]], axis=0)
    total_y = cells_y * lax.axis_size("gy")
    total_eddies = eddy_normal_cell.shape[0] * slab_count
    amplitude = math.sqrt(total_y * span / (total_eddies * SIGMA_Y * SIGMA_Z))
    eddy_weight = (2 * eddy_signs - 1).astype(jnp.float32) * eddy_strengths[:, None] * amplitude
    coords_y = (block_index * cells_y + jnp.arange(cells_y, dtype=jnp.int32)).astype(jnp.float32)
    coords_z = jnp.arange(span, dtype=jnp.int32).astype(jnp.float32)
    partial_sum = inflow_from(
        eddy_normal_cell.astype(jnp.float32),
        eddy_spanwise_cell.astype(jnp.float32),
        eddy_weight,
        coords_y,
        coords_z,
        span,
    )
    inflow = lax.psum(partial_sum, "gx")
    ghost_cells = ghost_state(inflow)
    padded = extended(fields, (("gx", 1), ("gy", 3)), 1)
    padded = padded.at[:, 0, :, 1:-1].set(
        jnp.where(slab_index == 0, ghost_cells, padded[:, 0, :, 1:-1])
    )
    padded = padded.at[:, -1, :, 1:-1].set(
        jnp.where(slab_index == slab_count - 1, fields[:, -1], padded[:, -1, :, 1:-1])
    )
    padded = padded.at[:, 1:-1, :, 0].set(
        jnp.where(block_index == 0, fields[:, :, :, 0], padded[:, 1:-1, :, 0])
    )
    padded = padded.at[:, 1:-1, :, -1].set(
        jnp.where(
            block_index == lax.axis_size("gy") - 1, fields[:, :, :, -1], padded[:, 1:-1, :, -1]
        )
    )
    updated, shock_sensor = section_rhs(padded)
    block_len = filter_matrices.shape[1]
    filter_row = slab_index * cells_x // block_len
    mask_row = lax.dynamic_slice_in_dim(shock_switch, filter_row, 1, 0).astype(jnp.float32)
    weight = mask_row[None] * shock_sensor
    columns = span * cells_y
    stacked = updated.reshape(5, cells_x, columns)
    weight_flat = weight.reshape(1, cells_x, columns)
    pencil, pencil_weight = (
        lax.all_to_all(stacked, "gx", split_axis=2, concat_axis=1, tiled=True),
        lax.all_to_all(weight_flat, "gx", split_axis=2, concat_axis=1, tiled=True),
    )
    smooth = filter_lines(pencil, filter_matrices)
    returned = pencil + pencil_weight * (smooth - pencil)
    back_lines = lax.all_to_all(returned, "gx", split_axis=1, concat_axis=2, tiled=True)
    conserved_next = back_lines.reshape(5, cells_x, span, cells_y)
    partial_histogram = plane_histogram(shock_sensor, dilatation_bin, vorticity_bin)
    summed = lax.psum(partial_histogram, ("gx", "gy"))
    all_cells = cells_x * slab_count * span * total_y
    histogram = summed * (HISTOGRAM_BINS * HISTOGRAM_BINS / all_cells)
    return (conserved_next, histogram)


def solution(mesh):
    in_specs = (
        P("gx", None, "gy"),
        P(None, "gx", None, "gy"),
        P("gx", None, "gy"),
        P("gx"),
        P("gx"),
        P("gx", None),
        P("gx"),
        P(),
        P(None, "gy"),
        P("gx", None, "gy"),
        P("gx", None, "gy"),
    )
    out_specs = (P(None, "gx", None, "gy"), P())
    return jax.shard_map(shards, mesh=mesh, in_specs=in_specs, out_specs=out_specs, check_vma=False)
```

profile of v0, /device:TPU:0, one launch (start us, length us, event | category | flops | bytes accessed | tf_op | source)
XLA Modules:
  0.0 215.9 jit_solution(9551707045615207745)
XLA Ops:
  1.6 1.3 collective-permute-start.1
  2.9 5.5 %collective-permute-start = (f32[5,1,32,32]{3,2,0,1:T(8,128)S(1)}, f32[5,1,32,32]{3,2,0,1:T(8,128)S(1)}, u32[]{:S(2)}, u32[]{:S(2)}) collective-permute-start(f32[5,1,32,32]{3,2,0,1:T(8,128)S(1)} %get-tuple-element.222), channel_id=1, source_target_pairs={{0,2},{2,4},{4,6},{6,8},{8,10},{10,12},{12,14},{14,16},{16,18},{18... | collective-permute-start | bytes 61448 | tf_op jit(solution)/shard_map/ppermute | solution.py:23
  10.8 75.6 %psum.14 = f32[3,32,32]{2,1,0:T(8,128)S(1)} all-reduce(f32[3,32,32]{2,1,0:T(8,128)S(1)} %fusion.50), channel_id=1, replica_groups=mesh['gx'=16,'gy'=2] {'gx'}, use_global_device_ids=true, to_apply=%region_1.2 | all-reduce | flops 3072 | bytes 24576 | tf_op jit(solution)/shard_map/psum | solution.py:153
  91.2 1.3 collective-permute-start.3
  92.5 3.0 %collective-permute-start.2 = (f32[5,10,32,1]{2,3,1,0:T(1,128)S(1)}, f32[5,10,32,1]{2,3,1,0:T(1,128)S(1)}, u32[]{:S(2)}, u32[]{:S(2)}) collective-permute-start(f32[5,10,32,1]{2,3,1,0:T(1,128)S(1)} %copy.81), channel_id=1, source_target_pairs={{0,1},{2,3},{4,5},{6,7},{8,9},{10,11},{12,13},{14,15},{16,17},{18,... | collective-permute-start | bytes 19208 | tf_op jit(solution)/shard_map/ppermute | solution.py:23
  95.5 1.4 and_reduce_fusion
  97.3 1.3 copy.84
  98.6 1.6 pad_maximum_fusion.1
  100.2 1.4 fusion.48
  101.6 1.7 scatter.14
  105.9 3.7 %scatter.19 = f32[5,10,32,34]{3,2,0,1:T(8,128)S(1)} dynamic-update-slice(f32[5,10,32,34]{3,2,0,1:T(8,128)S(1)} %scatter.16, f32[5,8,32,1]{3,2,0,1:T(8,128)S(1)} %slice_select_fusion, s32[]{:T(128)} %constant.328.clone.1, s32[]{:T(128)} %constant.350.clone.1, s32[]{:T(128)} %constant.328.clone.1, s32[]{:T(128)} %constant.351.clone.1) | dynamic-update-slice | bytes 10244 | tf_op jit(solution)/shard_map/scatter | solution.py:165
  114.4 3.7 %reduce.27 = f32[1024,8]{1,0:T(8,128)} reduce(f32[1024,1,8]{2,1,0:T(1,128)} %bitcast.128, f32[]{:T(128)} %broadcast.273), dimensions={1}, to_apply=%bitcast.110.reduce_sub_computation | reduce | bytes 65540
  118.1 1.9 reshape.467
  120.0 3.5 %all-to-all-start.1 = ((f32[16,1,512]{2,1,0:T(1,128)}), f32[16,1,512]{2,1,0:T(1,128)S(1)}, u32[]{:S(2)}, u32[]{:S(2)}) async-start(f32[16,1,512]{2,1,0:T(1,128)} %reshape.467), calls=%async_computation.1 | async-start | bytes 65536 | tf_op jit(solution)/shard_map/all_to_all | solution.py:180
  123.5 2.7 %fusion.14 = f32[5,8,32,32]{3,2,0,1:T(8,128)} fusion(f32[5,10,32,34]{3,2,0,1:T(8,128)S(1)} %get-tuple-element.221, f32[5,10,32,34]{3,2,0,1:T(8,128)S(1)} %scatter.19, f32[5,8,1,32]{3,2,0,1:T(1,128)S(1)} %get-tuple-element.213, f32[5,8,31,32]{3,2,0,1:T(8,128)} %get-tuple-element.215, f32[5,8,31,32]{3,2,0,1:T(8,128)S(1)} %get-tuple-element.214, ...), kind=kLoop, calls=%fused_computation.23 | loop fusion | flops 368640 | bytes 4295680 | tf_op jit(solution)/shard_map/sub | solution.py:75
  126.2 3.6 %copy.122 = f32[5,8,32,32]{1,0,3,2:T(8,128)} copy(f32[5,8,32,32]{3,2,0,1:T(8,128)} %fusion.14) | data formatting | bytes 327680 | tf_op jit(solution)/shard_map/reshape | solution.py:176
  129.8 3.4 %reshape.465 = f32[16,1,2560]{2,1,0:T(1,128)} reshape(f32[1024,5,8]{2,1,0:T(8,128)} %bitcast.117) | data formatting | bytes 327680
  133.1 6.9 %all-to-all-start = ((f32[16,1,2560]{2,1,0:T(1,128)}), f32[16,1,2560]{2,1,0:T(1,128)S(1)}, u32[]{:S(2)}, u32[]{:S(2)}) async-start(f32[16,1,2560]{2,1,0:T(1,128)} %reshape.465), calls=%async_computation | async-start | bytes 327680 | tf_op jit(solution)/shard_map/all_to_all | solution.py:179
  141.8 6.1 %all-to-all-done = f32[16,1,2560]{2,1,0:T(1,128)S(1)} async-done(((f32[16,1,2560]{2,1,0:T(1,128)}), f32[16,1,2560]{2,1,0:T(1,128)S(1)}, u32[]{:S(2)}, u32[]{:S(2)}) %all-to-all-start) | async-done | bytes 163872 | tf_op jit(solution)/shard_map/all_to_all | solution.py:179
  148.9 2.6 %reshape.466 = f32[1024,5,8]{2,1,0:T(8,128)} reshape(f32[16,2560]{1,0:T(8,128)S(1)} %reduce.26) | data formatting | bytes 327680
  151.5 2.6 %copy.103 = f32[5,16,8,64]{3,2,1,0:T(8,128)S(1)} copy(f32[5,16,8,64]{2,0,3,1:T(8,128)} %bitcast.118) | data formatting | bytes 327680 | tf_op jit(solution)/shard_map/all_to_all | solution.py:179
  156.1 3.5 %all-to-all-start.2 = ((f32[16,1,2560]{2,1,0:T(1,128)}), f32[16,1,2560]{2,1,0:T(1,128)S(1)}, u32[]{:S(2)}, u32[]{:S(2)}) async-start(f32[16,1,2560]{2,1,0:T(1,128)} %reshape.469), calls=%async_computation.2 | async-start | bytes 327680 | tf_op jit(solution)/shard_map/all_to_all | solution.py:184
  159.6 12.6 %while.22 = (s32[]{:T(128)}, f32[64,64]{1,0:T(8,128)S(1)}, s32[8,32,32]{2,1,0:T(8,128)}, s32[8,32,32]{2,1,0:T(8,128)}, f32[8,32,32]{2,1,0:T(8,128)S(1)}, /*index=5*/s32[]{:T(128)}, s32[]{:T(128)}) while((s32[]{:T(128)}, f32[64,64]{1,0:T(8,128)S(1)}, s32[8,32,32]{2,1,0:T(8,128)}, s32[8,32,32]{2,1,0:T(8,128)}, ...), condition=%wide.region_4.5_spmd.clone.clone, body=%wide.region_3.4_spmd.clone.clone.sunk | while | flops 50536448 | bytes 94311 | solution.py:113
  172.2 40.8 %psum.15 = f32[64,64]{1,0:T(8,128)S(1)} all-reduce(f32[64,64]{1,0:T(8,128)S(1)} %get-tuple-element.157), channel_id=1, replica_groups=mesh['gx'=16,'gy'=2] {'gx','gy'}, use_global_device_ids=true, to_apply=%region_5.6 | all-reduce | flops 4096 | bytes 32768 | tf_op jit(solution)/shard_map/psum | solution.py:187
  (125 shorter events, 35.6 us)
Async XLA Ops:
  0.6 153.6 %copy-start = (f32[1,128,128]{2,1,0:T(8,128)S(1)}, f32[1,128,128]{2,1,0:T(8,128)}, u32[]{:S(2)}) copy-start(f32[1,128,128]{2,1,0:T(8,128)} %param.40) | copy-start | bytes 196612
  1.6 93.9 %copy-start.4 = (s32[4]{0:T(128)S(1)}, s32[4]{0:T(128)}, u32[]{:S(2)}) copy-start(s32[4]{0:T(128)} %constant.330.clone.1) | copy-start | bytes 52
  1.6 87.3 %collective-permute-start.1 = (f32[5,1,32,32]{3,2,0,1:T(8,128)S(1)}, f32[5,1,32,32]{3,2,0,1:T(8,128)S(1)}, u32[]{:S(2)}, u32[]{:S(2)}) collective-permute-start(f32[5,1,32,32]{3,2,0,1:T(8,128)S(1)} %get-tuple-element.223), channel_id=1, source_target_pairs={{2,0},{4,2},{6,4},{8,6},{10,8},{12,10},{14,12},{16,14},{18,16},{20... | collective-permute-start | bytes 61448 | tf_op jit(solution)/shard_map/ppermute | solution.py:24
  2.9 86.0 %collective-permute-start = (f32[5,1,32,32]{3,2,0,1:T(8,128)S(1)}, f32[5,1,32,32]{3,2,0,1:T(8,128)S(1)}, u32[]{:S(2)}, u32[]{:S(2)}) collective-permute-start(f32[5,1,32,32]{3,2,0,1:T(8,128)S(1)} %get-tuple-element.222), channel_id=1, source_target_pairs={{0,2},{2,4},{4,6},{6,8},{8,10},{10,12},{12,14},{14,16},{16,18},{18... | collective-permute-start | bytes 61448 | tf_op jit(solution)/shard_map/ppermute | solution.py:23
  87.6 11.0 %copy-start.1 = (f32[3,8,32,32]{3,2,1,0:T(8,128)S(1)}, f32[3,8,32,32]{3,2,1,0:T(8,128)}, u32[]{:S(2)}) copy-start(f32[3,8,32,32]{3,2,1,0:T(8,128)} %param.34) | copy-start | bytes 294916
  87.6 11.0 %copy-start.2 = (f32[8,32,32]{2,1,0:T(8,128)S(1)}, f32[8,32,32]{2,1,0:T(8,128)}, u32[]{:S(2)}) copy-start(f32[8,32,32]{2,1,0:T(8,128)} %param.35) | copy-start | bytes 98308
  87.6 11.0 %copy-start.3 = (f32[8,32,32]{2,1,0:T(8,128)S(1)}, f32[8,32,32]{2,1,0:T(8,128)}, u32[]{:S(2)}) copy-start(f32[8,32,32]{2,1,0:T(8,128)} %param.33) | copy-start | bytes 98308
  91.2 6.1 %collective-permute-start.3 = (f32[5,10,32,1]{2,3,1,0:T(1,128)S(1)}, f32[5,10,32,1]{2,3,1,0:T(1,128)S(1)}, u32[]{:S(2)}, u32[]{:S(2)}) collective-permute-start(f32[5,10,32,1]{2,3,1,0:T(1,128)S(1)} %copy.82), channel_id=1, source_target_pairs={{1,0},{3,2},{5,4},{7,6},{9,8},{11,10},{13,12},{15,14},{17,16},{19,... | collective-permute-start | bytes 19208 | tf_op jit(solution)/shard_map/ppermute | solution.py:24
  92.5 4.4 %collective-permute-start.2 = (f32[5,10,32,1]{2,3,1,0:T(1,128)S(1)}, f32[5,10,32,1]{2,3,1,0:T(1,128)S(1)}, u32[]{:S(2)}, u32[]{:S(2)}) collective-permute-start(f32[5,10,32,1]{2,3,1,0:T(1,128)S(1)} %copy.81), channel_id=1, source_target_pairs={{0,1},{2,3},{4,5},{6,7},{8,9},{10,11},{12,13},{14,15},{16,17},{18,... | collective-permute-start | bytes 19208 | tf_op jit(solution)/shard_map/ppermute | solution.py:23
  120.0 13.2 %all-to-all-start.1 = ((f32[16,1,512]{2,1,0:T(1,128)}), f32[16,1,512]{2,1,0:T(1,128)S(1)}, u32[]{:S(2)}, u32[]{:S(2)}) async-start(f32[16,1,512]{2,1,0:T(1,128)} %reshape.467), calls=%async_computation.1 | async-start | bytes 65536 | tf_op jit(solution)/shard_map/all_to_all | solution.py:180
  133.1 14.8 %all-to-all-start = ((f32[16,1,2560]{2,1,0:T(1,128)}), f32[16,1,2560]{2,1,0:T(1,128)S(1)}, u32[]{:S(2)}, u32[]{:S(2)}) async-start(f32[16,1,2560]{2,1,0:T(1,128)} %reshape.465), calls=%async_computation | async-start | bytes 327680 | tf_op jit(solution)/shard_map/all_to_all | solution.py:179
  156.1 57.5 %all-to-all-start.2 = ((f32[16,1,2560]{2,1,0:T(1,128)}), f32[16,1,2560]{2,1,0:T(1,128)S(1)}, u32[]{:S(2)}, u32[]{:S(2)}) async-start(f32[16,1,2560]{2,1,0:T(1,128)} %reshape.469), calls=%async_computation.2 | async-start | bytes 327680 | tf_op jit(solution)/shard_map/all_to_all | solution.py:184
where the time goes:
time: 218 us; the launch traced here: 216 us
  blocking collectives  116 us (53%)
  local copies, waits for them, and re-layouts  39.7 us (18%)
  starting transfers between devices  25 us (11%)
  other arithmetic  21.8 us (10%)
  waiting for transfers between devices  6.13 us (3%)
  matrix products  5.55 us (3%)
    psum x1, blocking collectives, shards(): inflow = lax.psum(partial_sum, 'gx')  75.6 us
    psum x1, blocking collectives, shards(): summed = lax.psum(partial_histogram, ('gx', 'gy'))  40.8 us
    unnamed x16, local copies, waits for them, and re-layouts  9.82 us
    ppermute x2, starting transfers between devices, extended(): before = lax.ppermute(last, axis, up)  8.5 us
    all_to_all x1, starting transfers between devices, shards(): lax.all_to_all(stacked, 'gx', split_axis=2, concat_axis=1, tiled=True)  6.88 us
    all_to_all x1, waiting for transfers between devices, shards(): lax.all_to_all(stacked, 'gx', split_axis=2, concat_axis=1, tiled=True)  6.11 us
    dynamic_slice x16, local copies, waits for them, and re-layouts, plane_histogram(): lax.scan(accumulate_plane, jnp.zeros((HISTOGRAM_BINS, HISTOGRAM_BINS), jn...  6 us
    dot_general x8, matrix products, accumulate_plane(): jnp.dot(dilatation_table, vorticity_table, precision=lax.Precision.HIGHEST)  4.61 us
  transfers between devices with their start and end apart: 7, of which 1 were waited for; matrix products, arithmetic and copies ran while one was open for 14% of the time, Pallas kernels for 0%

commit v1 on v0

--- a/solution.py
+++ b/solution.py
@@ -184,7 +184,7 @@
     back_lines = lax.all_to_all(returned, "gx", split_axis=1, concat_axis=2, tiled=True)
     conserved_next = back_lines.reshape(5, cells_x, span, cells_y)
     partial_histogram = plane_histogram(shock_sensor, dilatation_bin, vorticity_bin)
-    summed = lax.psum(partial_histogram, ("gx", "gy"))
+    summed = jnp.sum(lax.all_gather(partial_histogram, ("gx", "gy")), 0)
     all_cells = cells_x * slab_count * span * total_y
     histogram = summed * (HISTOGRAM_BINS * HISTOGRAM_BINS / all_cells)
     return (conserved_next, histogram)

time: 218 us -> 219 us (level)
  waiting for transfers between devices: 6.13 us -> 0.03 us
  blocking collectives: 116 us -> 120 us
  starting transfers between devices: 25 us -> 28.4 us
    all_gather x0 -> x1, blocking collectives: none -> 44.6 us  [shards(): summed = jnp.sum(lax.all_gather(partial_histogram, ('gx', 'gy')), 0)]
    psum x1 -> x0, blocking collectives: 40.8 us -> none  [shards(): summed = lax.psum(partial_histogram, ('gx', 'gy'))]
    all_to_all x1, waiting for transfers between devices: 6.11 us -> 0.01 us  [shards(): lax.all_to_all(stacked, 'gx', split_axis=2, concat_axis=1, tiled=True)]
    all_to_all x1, starting transfers between devices: 3.52 us -> 6.9 us  [shards(): lax.all_to_all(returned, 'gx', split_axis=1, concat_axis=2, tiled=True)]
  transfers between devices with their start and end apart: 7 -> 7, of which waited for: 1 -> 0; matrix products, arithmetic and copies ran while one was open for 14% -> 14% of each run, Pallas kernels for 0% -> 0%
where the time goes in v1:
time: 219 us; the launch traced here: 217 us
  blocking collectives  120 us (55%)
  local copies, waits for them, and re-layouts  39.7 us (18%)
  starting transfers between devices  28.4 us (13%)
  other arithmetic  21.9 us (10%)
  matrix products  5.55 us (3%)
    psum x1, blocking collectives, shards(): inflow = lax.psum(partial_sum, 'gx')  75.6 us
    all_gather x1, blocking collectives, shards(): summed = jnp.sum(lax.all_gather(partial_histogram, ('gx', 'gy')), 0)  44.6 us
    unnamed x16, local copies, waits for them, and re-layouts  9.82 us
    ppermute x2, starting transfers between devices, extended(): before = lax.ppermute(last, axis, up)  8.5 us
    all_to_all x1, starting transfers between devices, shards(): lax.all_to_all(returned, 'gx', split_axis=1, concat_axis=2, tiled=True)  6.9 us
    all_to_all x1, starting transfers between devices, shards(): lax.all_to_all(stacked, 'gx', split_axis=2, concat_axis=1, tiled=True)  6.88 us
    dynamic_slice x16, local copies, waits for them, and re-layouts, plane_histogram(): lax.scan(accumulate_plane, jnp.zeros((HISTOGRAM_BINS, HISTOGRAM_BINS), jn...  5.97 us
    dot_general x8, matrix products, accumulate_plane(): jnp.dot(dilatation_table, vorticity_table, precision=lax.Precision.HIGHEST)  4.61 us
  transfers between devices with their start and end apart: 7, of which 0 were waited for; matrix products, arithmetic and copies ran while one was open for 14% of the time, Pallas kernels for 0%

profile of v1, /device:TPU:0, one launch (start us, length us, event | category | flops | bytes accessed | tf_op | source)
XLA Modules:
  0.0 217.1 jit_solution(7486132180842037127)
XLA Ops:
  1.6 1.3 collective-permute-start.1
  2.9 5.5 %collective-permute-start = (f32[5,1,32,32]{3,2,0,1:T(8,128)S(1)}, f32[5,1,32,32]{3,2,0,1:T(8,128)S(1)}, u32[]{:S(2)}, u32[]{:S(2)}) collective-permute-start(f32[5,1,32,32]{3,2,0,1:T(8,128)S(1)} %get-tuple-element.222), channel_id=1, source_target_pairs={{0,2},{2,4},{4,6},{6,8},{8,10},{10,12},{12,14},{14,16},{16,18},{18... | collective-permute-start | bytes 61448 | tf_op jit(solution)/shard_map/ppermute | solution.py:23
  10.8 75.6 %psum.7 = f32[3,32,32]{2,1,0:T(8,128)S(1)} all-reduce(f32[3,32,32]{2,1,0:T(8,128)S(1)} %fusion.50), channel_id=1, replica_groups=mesh['gx'=16,'gy'=2] {'gx'}, use_global_device_ids=true, to_apply=%region_1.2 | all-reduce | flops 3072 | bytes 24576 | tf_op jit(solution)/shard_map/psum | solution.py:153
  91.2 1.3 collective-permute-start.3
  92.5 3.0 %collective-permute-start.2 = (f32[5,10,32,1]{2,3,1,0:T(1,128)S(1)}, f32[5,10,32,1]{2,3,1,0:T(1,128)S(1)}, u32[]{:S(2)}, u32[]{:S(2)}) collective-permute-start(f32[5,10,32,1]{2,3,1,0:T(1,128)S(1)} %copy.81), channel_id=1, source_target_pairs={{0,1},{2,3},{4,5},{6,7},{8,9},{10,11},{12,13},{14,15},{16,17},{18,... | collective-permute-start | bytes 19208 | tf_op jit(solution)/shard_map/ppermute | solution.py:23
  95.5 1.4 and_reduce_fusion
  97.3 1.3 copy.84
  98.6 1.6 pad_maximum_fusion.1
  100.2 1.4 fusion.48
  101.6 1.7 scatter.14
  105.9 3.7 %scatter.19 = f32[5,10,32,34]{3,2,0,1:T(8,128)S(1)} dynamic-update-slice(f32[5,10,32,34]{3,2,0,1:T(8,128)S(1)} %scatter.16, f32[5,8,32,1]{3,2,0,1:T(8,128)S(1)} %slice_select_fusion, s32[]{:T(128)} %constant.328.clone.1, s32[]{:T(128)} %constant.350.clone.1, s32[]{:T(128)} %constant.328.clone.1, s32[]{:T(128)} %constant.351.clone.1) | dynamic-update-slice | bytes 10244 | tf_op jit(solution)/shard_map/scatter | solution.py:165
  111.2 1.2 fusion.91
  114.4 3.7 %reduce.27 = f32[1024,8]{1,0:T(8,128)} reduce(f32[1024,1,8]{2,1,0:T(1,128)} %bitcast.130, f32[]{:T(128)} %broadcast.273), dimensions={1}, to_apply=%bitcast.111.reduce_sub_computation | reduce | bytes 65540
  118.1 1.9 reshape.468
  120.0 3.5 %all-to-all-start.1 = ((f32[16,1,512]{2,1,0:T(1,128)}), f32[16,1,512]{2,1,0:T(1,128)S(1)}, u32[]{:S(2)}, u32[]{:S(2)}) async-start(f32[16,1,512]{2,1,0:T(1,128)} %reshape.468), calls=%async_computation.1 | async-start | bytes 65536 | tf_op jit(solution)/shard_map/all_to_all | solution.py:180
  123.5 2.7 %fusion.14 = f32[5,8,32,32]{3,2,0,1:T(8,128)} fusion(f32[5,10,32,34]{3,2,0,1:T(8,128)S(1)} %get-tuple-element.221, f32[5,10,32,34]{3,2,0,1:T(8,128)S(1)} %scatter.19, f32[5,8,1,32]{3,2,0,1:T(1,128)S(1)} %get-tuple-element.213, f32[5,8,31,32]{3,2,0,1:T(8,128)} %get-tuple-element.215, f32[5,8,31,32]{3,2,0,1:T(8,128)S(1)} %get-tuple-element.214, ...), kind=kLoop, calls=%fused_computation.23 | loop fusion | flops 368640 | bytes 4295680 | tf_op jit(solution)/shard_map/sub | solution.py:75
  126.2 3.6 %copy.122 = f32[5,8,32,32]{1,0,3,2:T(8,128)} copy(f32[5,8,32,32]{3,2,0,1:T(8,128)} %fusion.14) | data formatting | bytes 327680 | tf_op jit(solution)/shard_map/reshape | solution.py:176
  129.8 3.4 %reshape.466 = f32[16,1,2560]{2,1,0:T(1,128)} reshape(f32[1024,5,8]{2,1,0:T(8,128)} %bitcast.118) | data formatting | bytes 327680
  133.1 6.9 %all-to-all-start = ((f32[16,1,2560]{2,1,0:T(1,128)}), f32[16,1,2560]{2,1,0:T(1,128)S(1)}, u32[]{:S(2)}, u32[]{:S(2)}) async-start(f32[16,1,2560]{2,1,0:T(1,128)} %reshape.466), calls=%async_computation | async-start | bytes 327680 | tf_op jit(solution)/shard_map/all_to_all | solution.py:179
  140.0 12.6 %while.22 = (s32[]{:T(128)}, f32[64,64]{1,0:T(8,128)S(1)}, s32[8,32,32]{2,1,0:T(8,128)}, s32[8,32,32]{2,1,0:T(8,128)}, f32[8,32,32]{2,1,0:T(8,128)S(1)}, /*index=5*/s32[]{:T(128)}, s32[]{:T(128)}) while((s32[]{:T(128)}, f32[64,64]{1,0:T(8,128)S(1)}, s32[8,32,32]{2,1,0:T(8,128)}, s32[8,32,32]{2,1,0:T(8,128)}, ...), condition=%wide.region_4.5_spmd.clone.clone, body=%wide.region_3.4_spmd.clone.clone.sunk | while | flops 50536448 | bytes 94311 | solution.py:113
  155.4 2.6 %reshape.467 = f32[1024,5,8]{2,1,0:T(8,128)} reshape(f32[16,2560]{1,0:T(8,128)S(1)} %reduce.26) | data formatting | bytes 327680
  158.0 2.6 %copy.103 = f32[5,16,8,64]{3,2,1,0:T(8,128)S(1)} copy(f32[5,16,8,64]{2,0,3,1:T(8,128)} %bitcast.119) | data formatting | bytes 327680 | tf_op jit(solution)/shard_map/all_to_all | solution.py:179
  162.6 6.9 %all-to-all-start.2 = ((f32[16,1,2560]{2,1,0:T(1,128)}), f32[16,1,2560]{2,1,0:T(1,128)S(1)}, u32[]{:S(2)}, u32[]{:S(2)}) async-start(f32[16,1,2560]{2,1,0:T(1,128)} %reshape.470), calls=%async_computation.2 | async-start | bytes 327680 | tf_op jit(solution)/shard_map/all_to_all | solution.py:184
  169.5 44.6 %all-gather = f32[2048,64]{1,0:T(8,128)S(1)} all-gather(f32[64,64]{1,0:T(8,128)S(1)} %get-tuple-element.157), channel_id=2, replica_groups=mesh['gx'=16,'gy'=2] {'gx','gy'}, dimensions={0}, use_global_device_ids=true | all-gather | bytes 540672 | tf_op jit(solution)/shard_map/all_gather | solution.py:187
  (126 shorter events, 34.4 us)
Async XLA Ops:
  0.6 160.1 %copy-start = (f32[1,128,128]{2,1,0:T(8,128)S(1)}, f32[1,128,128]{2,1,0:T(8,128)}, u32[]{:S(2)}) copy-start(f32[1,128,128]{2,1,0:T(8,128)} %param.40) | copy-start | bytes 196612
  1.6 93.9 %copy-start.4 = (s32[4]{0:T(128)S(1)}, s32[4]{0:T(128)}, u32[]{:S(2)}) copy-start(s32[4]{0:T(128)} %constant.330.clone.1) | copy-start | bytes 52
  1.6 87.3 %collective-permute-start.1 = (f32[5,1,32,32]{3,2,0,1:T(8,128)S(1)}, f32[5,1,32,32]{3,2,0,1:T(8,128)S(1)}, u32[]{:S(2)}, u32[]{:S(2)}) collective-permute-start(f32[5,1,32,32]{3,2,0,1:T(8,128)S(1)} %get-tuple-element.223), channel_id=1, source_target_pairs={{2,0},{4,2},{6,4},{8,6},{10,8},{12,10},{14,12},{16,14},{18,16},{20... | collective-permute-start | bytes 61448 | tf_op jit(solution)/shard_map/ppermute | solution.py:24
  2.9 86.0 %collective-permute-start = (f32[5,1,32,32]{3,2,0,1:T(8,128)S(1)}, f32[5,1,32,32]{3,2,0,1:T(8,128)S(1)}, u32[]{:S(2)}, u32[]{:S(2)}) collective-permute-start(f32[5,1,32,32]{3,2,0,1:T(8,128)S(1)} %get-tuple-element.222), channel_id=1, source_target_pairs={{0,2},{2,4},{4,6},{6,8},{8,10},{10,12},{12,14},{14,16},{16,18},{18... | collective-permute-start | bytes 61448 | tf_op jit(solution)/shard_map/ppermute | solution.py:23
  87.6 11.0 %copy-start.1 = (f32[3,8,32,32]{3,2,1,0:T(8,128)S(1)}, f32[3,8,32,32]{3,2,1,0:T(8,128)}, u32[]{:S(2)}) copy-start(f32[3,8,32,32]{3,2,1,0:T(8,128)} %param.34) | copy-start | bytes 294916
  87.6 11.0 %copy-start.2 = (f32[8,32,32]{2,1,0:T(8,128)S(1)}, f32[8,32,32]{2,1,0:T(8,128)}, u32[]{:S(2)}) copy-start(f32[8,32,32]{2,1,0:T(8,128)} %param.35) | copy-start | bytes 98308
  87.6 11.0 %copy-start.3 = (f32[8,32,32]{2,1,0:T(8,128)S(1)}, f32[8,32,32]{2,1,0:T(8,128)}, u32[]{:S(2)}) copy-start(f32[8,32,32]{2,1,0:T(8,128)} %param.33) | copy-start | bytes 98308
  91.2 6.1 %collective-permute-start.3 = (f32[5,10,32,1]{2,3,1,0:T(1,128)S(1)}, f32[5,10,32,1]{2,3,1,0:T(1,128)S(1)}, u32[]{:S(2)}, u32[]{:S(2)}) collective-permute-start(f32[5,10,32,1]{2,3,1,0:T(1,128)S(1)} %copy.82), channel_id=1, source_target_pairs={{1,0},{3,2},{5,4},{7,6},{9,8},{11,10},{13,12},{15,14},{17,16},{19,... | collective-permute-start | bytes 19208 | tf_op jit(solution)/shard_map/ppermute | solution.py:24
  92.5 4.4 %collective-permute-start.2 = (f32[5,10,32,1]{2,3,1,0:T(1,128)S(1)}, f32[5,10,32,1]{2,3,1,0:T(1,128)S(1)}, u32[]{:S(2)}, u32[]{:S(2)}) collective-permute-start(f32[5,10,32,1]{2,3,1,0:T(1,128)S(1)} %copy.81), channel_id=1, source_target_pairs={{0,1},{2,3},{4,5},{6,7},{8,9},{10,11},{12,13},{14,15},{16,17},{18,... | collective-permute-start | bytes 19208 | tf_op jit(solution)/shard_map/ppermute | solution.py:23
  120.0 13.2 %all-to-all-start.1 = ((f32[16,1,512]{2,1,0:T(1,128)}), f32[16,1,512]{2,1,0:T(1,128)S(1)}, u32[]{:S(2)}, u32[]{:S(2)}) async-start(f32[16,1,512]{2,1,0:T(1,128)} %reshape.468), calls=%async_computation.1 | async-start | bytes 65536 | tf_op jit(solution)/shard_map/all_to_all | solution.py:180
  133.1 21.3 %all-to-all-start = ((f32[16,1,2560]{2,1,0:T(1,128)}), f32[16,1,2560]{2,1,0:T(1,128)S(1)}, u32[]{:S(2)}, u32[]{:S(2)}) async-start(f32[16,1,2560]{2,1,0:T(1,128)} %reshape.466), calls=%async_computation | async-start | bytes 327680 | tf_op jit(solution)/shard_map/all_to_all | solution.py:179
  162.6 52.3 %all-to-all-start.2 = ((f32[16,1,2560]{2,1,0:T(1,128)}), f32[16,1,2560]{2,1,0:T(1,128)S(1)}, u32[]{:S(2)}, u32[]{:S(2)}) async-start(f32[16,1,2560]{2,1,0:T(1,128)} %reshape.470), calls=%async_computation.2 | async-start | bytes 327680 | tf_op jit(solution)/shard_map/all_to_all | solution.py:184
